TPU v7x, 512 devices: a whole 4x4x16 slice. The times are simulated.
512 devices in a mesh: grid: 32 (over x, y, core), band: 16 (over z).
Axes of the slice: x: 4, y: 4, z: 16, core: 2. Of those that a mesh axis runs over, the one named last changes fastest.
Arguments:
- orbitals: bfloat16 [32768, 512], P('grid', 'band'), may hold values from -6 to 6
- rotation: bfloat16 [512, 32768], P('grid', 'band'), may hold values from -0.25 to 0.25
Outputs:
- rotated: bfloat16 [32768, 32768], P('grid', 'band')
All inputs are finite; a program needn't handle non-finite values.
Results may differ from a plain program's by a relative error of at most 0.001.
Values may be sent and summed in bfloat16 or wider, within the bound.
No kernel may reach another device: no remote copies, remote signals or barrier semaphores. Data moves between devices by JAX's collectives and lax.ppermute only.
A program may use at most 64 MiB of HBM per device.

v0:
```python
import jax
import jax.numpy as jnp
from jax import lax
from jax.sharding import PartitionSpec as P

ALONE = 896


def spread(block, axis):
    n = lax.axis_size(axis)
    copies = jnp.broadcast_to(block[None], (n, *block.shape))
    return lax.all_to_all(copies, axis, 0, 0, tiled=True).reshape(-1, block.shape[1])


def on_device(orbitals, rotation):
    columns = orbitals.T
    all_rows = spread(rotation, "grid")
    rest = spread(columns[:, ALONE:], "band")
    main = lax.all_gather(columns[:, :ALONE], "band", axis=0, tiled=True)
    all_cols = jnp.concatenate([main, rest], axis=1)
    total = lax.dot_general(
        all_cols, all_rows, (((0,), (0,)), ((), ())), preferred_element_type=jnp.float32
    )
    return total.astype(jnp.bfloat16)


def solution(mesh):
    in_specs = (P("grid", "band"), P("grid", "band"))
    out_specs = P("grid", "band")
    return jax.shard_map(
        on_device, mesh=mesh, in_specs=in_specs, out_specs=out_specs, check_vma=False
    )
```

profile of v0, /device:TPU:2, one launch (start us, length us, event | category | flops | bytes accessed | tf_op | source)
XLA Modules:
  0.0 78.8 jit_solution(8730877428883429115)
XLA Ops:
  0.0 0.7 slice.9
  0.7 29.7 %all_to_all.10 = bf16[16,32,128]{2,1,0:T(8,128)(2,1)S(1)} all-to-all(bf16[16,32,128]{2,1,0:T(8,128)(2,1)S(1)} %broadcast_in_dim.4), channel_id=1, replica_groups=mesh['grid'=32,'band'=16] {'band'}, dimensions={0} | all-to-all | bytes 262144 | tf_op jit(solution)/shard_map/all_to_all | solution.py:12
  30.4 2.4 %broadcast_in_dim.5 = bf16[32,16,2048]{2,1,0:T(8,128)(2,1)} broadcast(bf16[16,2048]{1,0:T(8,128)(2,1)} %param.3), dimensions={1,2} | broadcast | bytes 2162688 | tf_op jit(solution)/shard_map/broadcast_in_dim | solution.py:11
  32.8 0.0 copy-start
  32.8 7.8 %all-to-all-start.1 = ((bf16[32,16,2048]{2,1,0:T(8,128)(2,1)}), bf16[32,16,2048]{2,1,0:T(8,128)(2,1)S(1)}, u32[]{:S(2)}, u32[]{:S(2)}) async-start(bf16[32,16,2048]{2,1,0:T(8,128)(2,1)} %broadcast_in_dim.5), calls=%async_computation.1 | async-start | bytes 4194304 | tf_op jit(solution)/shard_map/all_to_all | solution.py:12
  40.6 0.0 copy-done
  40.6 33.8 %all_gather.3 = bf16[512,896]{1,0:T(8,128)(2,1)S(1)} all-gather(bf16[32,896]{1,0:T(8,128)(2,1)S(1)} %slice.8), channel_id=1, replica_groups=mesh['grid'=32,'band'=16] {'band'}, dimensions={0}, use_global_device_ids=true | all-gather | bytes 974848 | tf_op jit(solution)/shard_map/all_gather | solution.py:19
  74.4 0.0 all-to-all-done.1
  74.4 4.4 %convolution_convert_fusion = bf16[1024,2048]{1,0:T(8,128)(2,1)} fusion(bf16[512,2048]{1,0:T(8,128)(2,1)S(1)} %bitcast.4, bf16[512,128]{1,0:T(8,128)(2,1)S(1)} %bitcast.5, bf16[512,896]{1,0:T(8,128)(2,1)S(1)} %all_gather.3), kind=kOutput, calls=%fused_computation | convolution fusion | flops 2151677952 | bytes 7340032 | tf_op jit(solution)/shard_map/dot_general | solution.py:21
  (2 shorter events, 0.0 us)
Async XLA Ops:
  32.8 7.8 %copy-start = (bf16[1024,32]{0,1:T(8,128)(2,1)S(1)}, bf16[1024,32]{0,1:T(8,128)(2,1)}, u32[]{:S(2)}) copy-start(bf16[1024,32]{0,1:T(8,128)(2,1)} %param.2) | copy-start | bytes 196612
  32.8 41.6 %all-to-all-start.1 = ((bf16[32,16,2048]{2,1,0:T(8,128)(2,1)}), bf16[32,16,2048]{2,1,0:T(8,128)(2,1)S(1)}, u32[]{:S(2)}, u32[]{:S(2)}) async-start(bf16[32,16,2048]{2,1,0:T(8,128)(2,1)} %broadcast_in_dim.5), calls=%async_computation.1 | async-start | bytes 4194304 | tf_op jit(solution)/shard_map/all_to_all | solution.py:12
where the time goes:
time: 79.2 us; the launch traced here: 78.8 us
  blocking collectives  63.5 us (80%)
  starting transfers between devices  7.76 us (10%)
  matrix products  4.39 us (6%)
  local copies, waits for them, and re-layouts  3.14 us (4%)
    all_gather x1, blocking collectives, on_device(): main = lax.all_gather(columns[:, :ALONE], 'band', axis=0, tiled=True)  33.8 us
    all_to_all x1, blocking collectives, spread(): lax.all_to_all(copies, axis, 0, 0, tiled=True).reshape(-1, block.shape[1])  29.7 us
    all_to_all x1, starting transfers between devices, spread(): lax.all_to_all(copies, axis, 0, 0, tiled=True).reshape(-1, block.shape[1])  7.76 us
    dot_general x1, matrix products, on_device(): lax.dot_general(all_cols, all_rows, (((0,), (0,)), ((), ())), preferred_e...  4.39 us
    broadcast_in_dim x2, local copies, waits for them, and re-layouts, spread(): copies = jnp.broadcast_to(block[None], (n, *block.shape))  2.43 us
  transfers between devices with their start and end apart: 1, of which 0 were waited for; matrix products, arithmetic and copies ran while one was open for 0% of the time, Pallas kernels for 0%

commit v1 on v0

--- a/solution.py
+++ b/solution.py
@@ -16,7 +16,10 @@
     columns = orbitals.T
     all_rows = spread(rotation, "grid")
     rest = spread(columns[:, ALONE:], "band")
-    main = lax.all_gather(columns[:, :ALONE], "band", axis=0, tiled=True)
+    main = jnp.concatenate(
+        lax.all_to_all(jnp.stack([columns[:, :ALONE]] * lax.axis_size("band")), "band", 0, 0),
+        axis=0,
+    )
     all_cols = jnp.concatenate([main, rest], axis=1)
     total = lax.dot_general(
         all_cols, all_rows, (((0,), (0,)), ((), ())), preferred_element_type=jnp.float32

time: 79.2 us -> 123 us (1.55)
  the two profiles are of different devices: /device:TPU:2 before, /device:TPU:4 now
where the time goes in v1:
time: 123 us; the launch traced here: 122 us
  blocking collectives  81 us (66%)
  waiting for transfers between devices  25.9 us (21%)
  starting transfers between devices  7.73 us (6%)
  matrix products  4.39 us (4%)
  local copies, waits for them, and re-layouts  3.21 us (3%)
    all_to_all x1, blocking collectives, on_device(): lax.all_to_all(jnp.stack([columns[:, :ALONE]] * lax.axis_size('band')), '...  51.3 us
    all_to_all x1, blocking collectives, spread(): lax.all_to_all(copies, axis, 0, 0, tiled=True).reshape(-1, block.shape[1])  29.7 us
    all_to_all x1, waiting for transfers between devices, spread(): lax.all_to_all(copies, axis, 0, 0, tiled=True).reshape(-1, block.shape[1])  25.9 us
    all_to_all x1, starting transfers between devices, spread(): lax.all_to_all(copies, axis, 0, 0, tiled=True).reshape(-1, block.shape[1])  7.73 us
    dot_general x1, matrix products, on_device(): lax.dot_general(all_cols, all_rows, (((0,), (0,)), ((), ())), preferred_e...  4.39 us
  transfers between devices with their start and end apart: 1, of which 1 were waited for; matrix products, arithmetic and copies ran while one was open for 0% of the time, Pallas kernels for 0%

profile of v1, /device:TPU:4, one launch (start us, length us, event | category | flops | bytes accessed | tf_op | source)
XLA Modules:
  0.0 122.3 jit_solution(8781690993555527606)
XLA Ops:
  0.0 0.7 slice.9
  0.7 29.7 %all_to_all.15 = bf16[16,32,128]{2,1,0:T(8,128)(2,1)S(1)} all-to-all(bf16[16,32,128]{2,1,0:T(8,128)(2,1)S(1)} %broadcast_in_dim.4), channel_id=1, replica_groups=mesh['grid'=32,'band'=16] {'band'}, dimensions={0} | all-to-all | bytes 262144 | tf_op jit(solution)/shard_map/all_to_all | solution.py:12
  30.4 2.4 %broadcast_in_dim.5 = bf16[32,16,2048]{2,1,0:T(8,128)(2,1)} broadcast(bf16[16,2048]{1,0:T(8,128)(2,1)} %param.3), dimensions={1,2} | broadcast | bytes 2162688 | tf_op jit(solution)/shard_map/broadcast_in_dim | solution.py:11
  32.8 0.0 copy-start
  32.8 7.7 %all-to-all-start.2 = ((bf16[32,16,2048]{2,1,0:T(8,128)(2,1)}), bf16[32,16,2048]{2,1,0:T(8,128)(2,1)S(1)}, u32[]{:S(2)}, u32[]{:S(2)}) async-start(bf16[32,16,2048]{2,1,0:T(8,128)(2,1)} %broadcast_in_dim.5), calls=%async_computation.2 | async-start | bytes 4194304 | tf_op jit(solution)/shard_map/all_to_all | solution.py:12
  40.6 0.0 copy-done
  40.6 25.9 %all-to-all-done.2 = bf16[32,16,2048]{2,1,0:T(8,128)(2,1)S(1)} async-done(((bf16[32,16,2048]{2,1,0:T(8,128)(2,1)}), bf16[32,16,2048]{2,1,0:T(8,128)(2,1)S(1)}, u32[]{:S(2)}, u32[]{:S(2)}) %all-to-all-start.2) | async-done | bytes 2097184 | tf_op jit(solution)/shard_map/all_to_all | solution.py:12
  66.5 0.1 stack.2
  66.6 51.3 %all_to_all.16 = bf16[16,32,896]{2,1,0:T(8,128)(2,1)S(1)} all-to-all(bf16[16,32,896]{2,1,0:T(8,128)(2,1)S(1)} %stack.2), channel_id=1, replica_groups=mesh['grid'=32,'band'=16] {'band'}, dimensions={0} | all-to-all | bytes 1835008 | tf_op jit(solution)/shard_map/all_to_all | solution.py:20
  117.9 4.4 %convolution_convert_fusion = bf16[1024,2048]{1,0:T(8,128)(2,1)} fusion(bf16[512,2048]{1,0:T(8,128)(2,1)S(1)} %bitcast.5, bf16[512,128]{1,0:T(8,128)(2,1)S(1)} %bitcast.7, bf16[512,896]{1,0:T(8,128)(2,1)S(1)} %bitcast.6), kind=kOutput, calls=%fused_computation | convolution fusion | flops 2151677952 | bytes 7340032 | tf_op jit(solution)/shard_map/dot_general | solution.py:24
  (2 shorter events, 0.0 us)
Async XLA Ops:
  32.8 7.7 %copy-start = (bf16[1024,32]{0,1:T(8,128)(2,1)S(1)}, bf16[1024,32]{0,1:T(8,128)(2,1)}, u32[]{:S(2)}) copy-start(bf16[1024,32]{0,1:T(8,128)(2,1)} %param.2) | copy-start | bytes 196612
  32.8 33.7 %all-to-all-start.2 = ((bf16[32,16,2048]{2,1,0:T(8,128)(2,1)}), bf16[32,16,2048]{2,1,0:T(8,128)(2,1)S(1)}, u32[]{:S(2)}, u32[]{:S(2)}) async-start(bf16[32,16,2048]{2,1,0:T(8,128)(2,1)} %broadcast_in_dim.5), calls=%async_computation.2 | async-start | bytes 4194304 | tf_op jit(solution)/shard_map/all_to_all | solution.py:12
